TPU v7x, 32 devices: a whole 2x2x4 slice. The times are simulated.
32 devices in a mesh: members: 4 (over y, core), space: 8 (over z, x).
Axes of the slice: x: 2, y: 2, z: 4, core: 2. Of those that a mesh axis runs over, the one named last changes fastest.
Arguments:
- ensemble: float32 [3, 512, 64, 256], P(None, 'members', 'space'), may hold values from -6 to 6
- obs_cells: int32 [8, 4, 128], P('space', 'members'), may hold values from 0 to 1535
- obs_values: float32 [8, 4, 128], P('space', 'members'), may hold values from -6 to 6
- obs_var: float32 [8, 4, 128], P('space', 'members'), may hold values from 0.25 to 4
- obs_noise: float32 [512, 8, 4, 128], P(None, 'space', 'members'), may hold values from -6 to 6
- assign: int32 [512], replicated, may hold values from 0 to 511, each once
Outputs:
- analysis: float32 [3, 512, 64, 256], P(None, 'members', 'space')
Inputs may be any that keep to these rules, and one draw needn't show every extreme that they name: assign holds every member once. obs_cells[r, c, k] = field * 8 * 64 + row * 64 + column within tile (r, c); repeats are possible.
All inputs are finite; a program needn't handle non-finite values.
Results may differ from a plain program's by a relative error of at most 0.0003.
Values sent between devices are 32-bit elements; how exact they have to be, the bound alone decides.
A program may use at most 64 MiB of HBM per device.

v0:
```python
import jax
import jax.numpy as jnp
from jax import lax
from jax.sharding import PartitionSpec as P

TILE_W = 64
STEPS = 4
tstep = 0.1
gravity = 1.0
depth = 1.0
coriolis = 0.25
viscosity = 0.5


def extended(cells, sides, width):
    for axis, dim in sides:
        count = lax.axis_size(axis)
        head = lax.slice_in_dim(cells, 0, width, axis=dim)
        tail = lax.slice_in_dim(cells, cells.shape[dim] - width, cells.shape[dim], axis=dim)
        cells = jnp.concatenate(
            [
                lax.ppermute(tail, axis, [(i, (i + 1) % count) for i in range(count)]),
                cells,
                lax.ppermute(head, axis, [((i + 1) % count, i) for i in range(count)]),
            ],
            axis=dim,
        )
    return cells


def centred_x(field):
    return 0.5 * (jnp.roll(field, -1, axis=2) - jnp.roll(field, 1, axis=2))


def height_update(state):
    eta, east, north = (state[0], state[1], state[2])
    column = depth + eta
    flux_x = centred_x(column * east)[:, 1:-1]
    carried = column * north
    flux_y = 0.5 * (carried[:, 2:] - carried[:, :-2])
    return eta[:, 1:-1] - tstep * (flux_x + flux_y)


def momentum_update(eta, east, north):

    def advance(field, extra):
        inner = field[:, 1:-1]
        grad_x = centred_x(field)[:, 1:-1]
        grad_y = 0.5 * (field[:, 2:] - field[:, :-2])
        spread = (
            jnp.roll(field, -1, axis=2)[:, 1:-1]
            + jnp.roll(field, 1, axis=2)[:, 1:-1]
            + field[:, 2:]
            + field[:, :-2]
            - 4.0 * inner
        )
        return inner + tstep * (
            -east[:, 1:-1] * grad_x - north[:, 1:-1] * grad_y + extra + viscosity * spread
        )

    slope_x = centred_x(eta)[:, 1:-1]
    slope_y = 0.5 * (eta[:, 2:] - eta[:, :-2])
    new_east = advance(east, coriolis * north[:, 1:-1] - gravity * slope_x)
    new_north = advance(north, -coriolis * east[:, 1:-1] - gravity * slope_y)
    return (new_east, new_north)


def thin_pad(state):
    return extended(state, (("space", 2),), 1)


def analyse_tile(tile, near):
    count = tile.shape[1]
    spread_all = jnp.transpose(near[:, :, 0], (2, 0, 1, 3)).reshape(count, -1)
    misfit_all = jnp.transpose(near[:, :, 1], (2, 0, 1, 3)).reshape(count, -1)
    gram = jnp.dot(spread_all, spread_all.T, precision=lax.Precision.HIGHEST) / (
        count - 1
    ) + jnp.eye(count, dtype=jnp.float32)
    factor = jnp.linalg.cholesky(gram)
    reduced = jax.scipy.linalg.cho_solve((factor, True), spread_all)
    mixing = jnp.dot(misfit_all, reduced.T, precision=lax.Precision.HIGHEST) / (count - 1)
    anomaly = tile - jnp.mean(tile, axis=1, keepdims=True)
    return tile + jnp.einsum("ij,fjc->fic", mixing, anomaly, precision=lax.Precision.HIGHEST)


def local(ensemble, obs_cells, obs_values, obs_var, obs_noise, assign):
    state = ensemble
    for step in range(STEPS):
        eta_new = height_update(thin_pad(state))
        padded = thin_pad(jnp.stack([eta_new, state[1], state[2]]))
        east, north = momentum_update(padded[0], padded[1], padded[2])
        state = jnp.stack([eta_new, east, north])
    width = TILE_W
    tiles = lax.all_to_all(state, "members", split_axis=3, concat_axis=1, tiled=True)
    count = tiles.shape[1]
    rows_here = tiles.shape[2]
    tile = tiles.reshape(3, count, rows_here * width)
    tile_cells = rows_here * width
    cells = obs_cells.reshape(-1)
    field_of = cells // tile_cells
    cell_of = cells % tile_cells
    shape = (3, tile_cells, cells.shape[0])
    pick = (
        (lax.broadcasted_iota(jnp.int32, shape, 0) == field_of[None, None, :])
        & (lax.broadcasted_iota(jnp.int32, shape, 1) == cell_of[None, None, :])
    ).astype(jnp.float32)
    observed = jnp.einsum("fmc,fco->mo", tile, pick, precision=lax.Precision.HIGHEST)
    scale = 1.0 / jnp.sqrt(obs_var.reshape(-1))
    mean_obs = jnp.mean(observed, axis=0, keepdims=True)
    spread = (observed - mean_obs) * scale
    noise = jnp.take(obs_noise.reshape(count, -1), assign, axis=0)
    misfit = (obs_values.reshape(-1)[None, :] - observed) * scale + noise
    packed = jnp.stack([spread, misfit])[None, None]
    near = extended(packed, (("members", 1), ("space", 0)), 1)
    updated = analyse_tile(tile, near).reshape(3, count, rows_here, width)
    return lax.all_to_all(updated, "members", split_axis=1, concat_axis=3, tiled=True)


def solution(mesh):
    in_specs = (
        P(None, "members", "space", None),
        P("space", "members", None),
        P("space", "members", None),
        P("space", "members", None),
        P(None, "space", "members", None),
        P(),
    )
    out_specs = P(None, "members", "space", None)
    return jax.shard_map(local, mesh=mesh, in_specs=in_specs, out_specs=out_specs, check_vma=False)
```

profile of v0, /device:TPU:0, one launch (start us, length us, event | category | flops | bytes accessed | tf_op | source)
XLA Modules:
  0.0 610.9 jit_solution(4791062386174462947)
XLA Ops:
  9.4 13.6 %collective-permute-done = f32[3,128,1,256]{1,2,3,0:T(1,128)S(1)} collective-permute-done((f32[3,128,1,256]{1,2,3,0:T(1,128)S(1)}, f32[3,128,1,256]{1,2,3,0:T(1,128)S(1)}, u32[]{:S(2)}, u32[]{:S(2)}) %collective-permute-start) | collective-permute-done | bytes 393248 | tf_op jit(solution)/shard_map/ppermute | solution.py:22
  33.1 11.5 %collective-permute-done.2 = f32[3,128,1,256]{1,2,3,0:T(1,128)S(1)} collective-permute-done((f32[3,128,1,256]{1,2,3,0:T(1,128)S(1)}, f32[3,128,1,256]{1,2,3,0:T(1,128)S(1)}, u32[]{:S(2)}, u32[]{:S(2)}) %collective-permute-start.2) | collective-permute-done | bytes 393248 | tf_op jit(solution)/shard_map/ppermute | solution.py:22
  60.4 11.6 %collective-permute-done.4 = f32[3,128,1,256]{1,2,3,0:T(1,128)S(1)} collective-permute-done((f32[3,128,1,256]{1,2,3,0:T(1,128)S(1)}, f32[3,128,1,256]{1,2,3,0:T(1,128)S(1)}, u32[]{:S(2)}, u32[]{:S(2)}) %collective-permute-start.4) | collective-permute-done | bytes 393248 | tf_op jit(solution)/shard_map/ppermute | solution.py:22
  84.6 11.7 %collective-permute-done.6 = f32[3,128,1,256]{1,2,3,0:T(1,128)S(1)} collective-permute-done((f32[3,128,1,256]{1,2,3,0:T(1,128)S(1)}, f32[3,128,1,256]{1,2,3,0:T(1,128)S(1)}, u32[]{:S(2)}, u32[]{:S(2)}) %collective-permute-start.6) | collective-permute-done | bytes 393248 | tf_op jit(solution)/shard_map/ppermute | solution.py:22
  111.9 11.7 %collective-permute-done.8 = f32[3,128,1,256]{1,2,3,0:T(1,128)S(1)} collective-permute-done((f32[3,128,1,256]{1,2,3,0:T(1,128)S(1)}, f32[3,128,1,256]{1,2,3,0:T(1,128)S(1)}, u32[]{:S(2)}, u32[]{:S(2)}) %collective-permute-start.8) | collective-permute-done | bytes 393248 | tf_op jit(solution)/shard_map/ppermute | solution.py:22
  135.0 10.5 %collective-permute-done.10 = f32[3,128,1,256]{1,2,3,0:T(1,128)S(1)} collective-permute-done((f32[3,128,1,256]{1,2,3,0:T(1,128)S(1)}, f32[3,128,1,256]{1,2,3,0:T(1,128)S(1)}, u32[]{:S(2)}, u32[]{:S(2)}) %collective-permute-start.10) | collective-permute-done | bytes 393248 | tf_op jit(solution)/shard_map/ppermute | solution.py:22
  162.0 12.4 %collective-permute-done.12 = f32[3,128,1,256]{1,2,3,0:T(1,128)S(1)} collective-permute-done((f32[3,128,1,256]{1,2,3,0:T(1,128)S(1)}, f32[3,128,1,256]{1,2,3,0:T(1,128)S(1)}, u32[]{:S(2)}, u32[]{:S(2)}) %collective-permute-start.12) | collective-permute-done | bytes 393248 | tf_op jit(solution)/shard_map/ppermute | solution.py:22
  186.0 11.5 %collective-permute-done.14 = f32[3,128,1,256]{1,2,3,0:T(1,128)S(1)} collective-permute-done((f32[3,128,1,256]{1,2,3,0:T(1,128)S(1)}, f32[3,128,1,256]{1,2,3,0:T(1,128)S(1)}, u32[]{:S(2)}, u32[]{:S(2)}) %collective-permute-start.14) | collective-permute-done | bytes 393248 | tf_op jit(solution)/shard_map/ppermute | solution.py:22
  217.2 33.3 %all-to-all-done = f32[3,128,8,256]{1,2,0,3:T(8,128)S(1)} async-done(((f32[3,128,8,256]{1,2,0,3:T(8,128)}), f32[3,128,8,256]{1,2,0,3:T(8,128)S(1)}, u32[]{:S(2)}, u32[]{:S(2)}) %all-to-all-start) | async-done | bytes 3145760 | tf_op jit(solution)/shard_map/all_to_all | solution.py:94
  263.4 11.2 %collective-permute-done.17 = f32[1,1,2,512,128]{3,4,2,1,0:T(8,128)S(1)} collective-permute-done((f32[1,1,2,512,128]{3,4,2,1,0:T(8,128)S(1)}, f32[1,1,2,512,128]{3,4,2,1,0:T(8,128)S(1)}, u32[]{:S(2)}, u32[]{:S(2)}) %collective-permute-start.17) | collective-permute-done | bytes 524320 | tf_op jit(solution)/shard_map/ppermute | solution.py:24
  284.9 63.5 %collective-permute-done.19 = f32[1,3,2,512,128]{3,4,2,1,0:T(8,128)} collective-permute-done((f32[1,3,2,512,128]{3,4,2,1,0:T(8,128)}, f32[1,3,2,512,128]{3,4,2,1,0:T(8,128)}, u32[]{:S(2)}, u32[]{:S(2)}) %collective-permute-start.19) | collective-permute-done | bytes 1572896 | tf_op jit(solution)/shard_map/ppermute | solution.py:24
  363.9 11.7 %cholesky.104 = f32[128,128]{1,0:T(8,128)S(1)} custom-call(f32[128,128]{1,0:T(8,128)S(1)} %cholesky.266), custom_call_target="Cholesky" | custom-call | tf_op jit(solution)/shard_map/jit(cholesky)/cholesky | solution.py:79
  381.1 10.2 %custom-call.34 = f32[1,128,128]{1,2,0:T(8,128)S(1)} custom-call(f32[1,128,128]{2,1,0:T(8,128)S(1)} %get-tuple-element.140), custom_call_target="InvertDiagBlocksLowerTriangular" | custom-call | tf_op jit(solution)/shard_map/jit(cholesky)/cholesky | solution.py:79
  396.2 11.7 %cholesky.217 = f32[128,128]{1,0:T(8,128)S(1)} custom-call(f32[128,128]{1,0:T(8,128)S(1)} %cholesky.270), custom_call_target="Cholesky" | custom-call | tf_op jit(solution)/shard_map/jit(cholesky)/cholesky | solution.py:79
  408.6 9.8 %custom-call.35 = f32[1,128,128]{1,2,0:T(8,128)S(1)} custom-call(f32[1,128,128]{2,1,0:T(8,128)S(1)} %get-tuple-element.137), custom_call_target="InvertDiagBlocksLowerTriangular" | custom-call | tf_op jit(solution)/shard_map/jit(cholesky)/cholesky | solution.py:79
  419.1 11.7 %cholesky.238 = f32[128,128]{1,0:T(8,128)S(1)} custom-call(f32[128,128]{1,0:T(8,128)S(1)} %cholesky.275), custom_call_target="Cholesky" | custom-call | tf_op jit(solution)/shard_map/jit(cholesky)/cholesky | solution.py:79
  431.6 9.9 %custom-call.36 = f32[1,128,128]{1,2,0:T(8,128)S(1)} custom-call(f32[1,128,128]{2,1,0:T(8,128)S(1)} %get-tuple-element.134), custom_call_target="InvertDiagBlocksLowerTriangular" | custom-call | tf_op jit(solution)/shard_map/jit(cholesky)/cholesky | solution.py:79
  442.1 11.7 %cholesky.255 = f32[128,128]{1,0:T(8,128)S(1)} custom-call(f32[128,128]{1,0:T(8,128)S(1)} %convolution_subtract_fusion.8), custom_call_target="Cholesky" | custom-call | tf_op jit(solution)/shard_map/jit(cholesky)/cholesky | solution.py:79
  457.1 10.6 %while.1 = (s32[]{:T(128)}, f32[512,512]{1,0:T(8,128)S(1)}, s32[4,2]{0,1:T(2,128)S(1)}, f32[4,128,128]{2,1,0:T(8,128)}, s32[]{:T(128)}) while((s32[]{:T(128)}, f32[512,512]{1,0:T(8,128)S(1)}, s32[4,2]{0,1:T(2,128)S(1)}, f32[4,128,128]{2,1,0:T(8,128)}, s32[]{:T(128)}) %tuple.90), condition=%wide.while_cond, body=%wide.while_body.sunk | while | flops 2 | bytes 132205 | solution.py:80
  467.7 40.3 %custom-call.37 = f32[4,128,128]{1,2,0:T(8,128)S(1)} custom-call(f32[4,128,128]{2,1,0:T(8,128)} %get-tuple-element.12), custom_call_target="InvertDiagBlocksLowerTriangular" | custom-call | tf_op jit(solution)/shard_map/jit(_cho_solve)/triangular_solve | solution.py:80
  533.5 7.0 %reshape.132 = f32[4,1,196608]{2,1,0:T(1,128)} reshape(f32[512,3,8,64]{3,2,1,0:T(8,128)} %bitcast.224) | data formatting | bytes 6291456
  540.6 40.7 %all_to_all.33 = f32[4,1,196608]{2,1,0:T(1,128)S(1)} all-to-all(f32[4,1,196608]{2,1,0:T(1,128)} %reshape.132), channel_id=1, replica_groups=mesh['members'=4,'space'=8] {'members'}, dimensions={0} | all-to-all | bytes 6291456 | tf_op jit(solution)/shard_map/all_to_all | solution.py:116
  581.9 10.6 %reduce.25 = f32[4,196608]{1,0:T(4,128)} reduce(f32[4,1,196608]{2,1,0:T(1,128)S(1)} %all_to_all.33, f32[]{:T(128)} %broadcast.379), dimensions={1}, to_apply=%all_to_all.27.reduce_sub_computation | reduce | bytes 6291460 | tf_op jit(solution)/shard_map/all_to_all | solution.py:116
  592.5 7.4 %reshape.133 = f32[512,3,8,64]{3,2,1,0:T(8,128)} reshape(f32[4,196608]{1,0:T(4,128)} %reduce.25) | data formatting | bytes 6291456
  (232 shorter events, 221.6 us)
Async XLA Ops:
  0.0 213.7 %copy-start = (f32[512,1,1,128]{3,2,1,0:T(1,128)S(1)}, f32[512,1,1,128]{3,2,1,0:T(1,128)}, u32[]{:S(2)}) copy-start(f32[512,1,1,128]{3,2,1,0:T(1,128)} %param.10) | copy-start | bytes 786436
  3.1 19.8 %collective-permute-start = (f32[3,128,1,256]{1,2,3,0:T(1,128)S(1)}, f32[3,128,1,256]{1,2,3,0:T(1,128)S(1)}, u32[]{:S(2)}, u32[]{:S(2)}) collective-permute-start(f32[3,128,1,256]{1,2,3,0:T(1,128)S(1)} %get-tuple-element.59), channel_id=1, source_target_pairs={{0,1},{1,2},{2,3},{3,4},{4,5},{5,6},{6,7},{7,0},{8,9},{9,10},{10,1... | collective-permute-start | bytes 1179656 | tf_op jit(solution)/shard_map/ppermute | solution.py:22
  6.1 19.0 %collective-permute-start.1 = (f32[3,128,1,256]{1,2,3,0:T(1,128)S(1)}, f32[3,128,1,256]{1,2,3,0:T(1,128)S(1)}, u32[]{:S(2)}, u32[]{:S(2)}) collective-permute-start(f32[3,128,1,256]{1,2,3,0:T(1,128)S(1)} %get-tuple-element.60), channel_id=1, source_target_pairs={{1,0},{2,1},{3,2},{4,3},{5,4},{6,5},{7,6},{0,7},{9,8},{10,9},{11,1... | collective-permute-start | bytes 1179656 | tf_op jit(solution)/shard_map/ppermute | solution.py:24
  28.4 16.3 %collective-permute-start.2 = (f32[3,128,1,256]{1,2,3,0:T(1,128)S(1)}, f32[3,128,1,256]{1,2,3,0:T(1,128)S(1)}, u32[]{:S(2)}, u32[]{:S(2)}) collective-permute-start(f32[3,128,1,256]{1,2,3,0:T(1,128)S(1)} %get-tuple-element.57), channel_id=1, source_target_pairs={{0,1},{1,2},{2,3},{3,4},{4,5},{5,6},{6,7},{7,0},{8,9},{9,10},{10,1... | collective-permute-start | bytes 1179656 | tf_op jit(solution)/shard_map/ppermute | solution.py:22
  28.7 19.9 %collective-permute-start.3 = (f32[3,128,1,256]{1,2,3,0:T(1,128)S(1)}, f32[3,128,1,256]{1,2,3,0:T(1,128)S(1)}, u32[]{:S(2)}, u32[]{:S(2)}) collective-permute-start(f32[3,128,1,256]{1,2,3,0:T(1,128)S(1)} %get-tuple-element.58), channel_id=1, source_target_pairs={{1,0},{2,1},{3,2},{4,3},{5,4},{6,5},{7,6},{0,7},{9,8},{10,9},{11,1... | collective-permute-start | bytes 1179656 | tf_op jit(solution)/shard_map/ppermute | solution.py:24
  55.3 16.6 %collective-permute-start.4 = (f32[3,128,1,256]{1,2,3,0:T(1,128)S(1)}, f32[3,128,1,256]{1,2,3,0:T(1,128)S(1)}, u32[]{:S(2)}, u32[]{:S(2)}) collective-permute-start(f32[3,128,1,256]{1,2,3,0:T(1,128)S(1)} %get-tuple-element.55), channel_id=1, source_target_pairs={{0,1},{1,2},{2,3},{3,4},{4,5},{5,6},{6,7},{7,0},{8,9},{9,10},{10,1... | collective-permute-start | bytes 1179656 | tf_op jit(solution)/shard_map/ppermute | solution.py:22
  55.4 20.6 %collective-permute-start.5 = (f32[3,128,1,256]{1,2,3,0:T(1,128)S(1)}, f32[3,128,1,256]{1,2,3,0:T(1,128)S(1)}, u32[]{:S(2)}, u32[]{:S(2)}) collective-permute-start(f32[3,128,1,256]{1,2,3,0:T(1,128)S(1)} %get-tuple-element.56), channel_id=1, source_target_pairs={{1,0},{2,1},{3,2},{4,3},{5,4},{6,5},{7,6},{0,7},{9,8},{10,9},{11,1... | collective-permute-start | bytes 1179656 | tf_op jit(solution)/shard_map/ppermute | solution.py:24
  79.9 16.5 %collective-permute-start.6 = (f32[3,128,1,256]{1,2,3,0:T(1,128)S(1)}, f32[3,128,1,256]{1,2,3,0:T(1,128)S(1)}, u32[]{:S(2)}, u32[]{:S(2)}) collective-permute-start(f32[3,128,1,256]{1,2,3,0:T(1,128)S(1)} %get-tuple-element.53), channel_id=1, source_target_pairs={{0,1},{1,2},{2,3},{3,4},{4,5},{5,6},{6,7},{7,0},{8,9},{9,10},{10,1... | collective-permute-start | bytes 1179656 | tf_op jit(solution)/shard_map/ppermute | solution.py:22
  79.9 20.1 %collective-permute-start.7 = (f32[3,128,1,256]{1,2,3,0:T(1,128)S(1)}, f32[3,128,1,256]{1,2,3,0:T(1,128)S(1)}, u32[]{:S(2)}, u32[]{:S(2)}) collective-permute-start(f32[3,128,1,256]{1,2,3,0:T(1,128)S(1)} %get-tuple-element.54), channel_id=1, source_target_pairs={{1,0},{2,1},{3,2},{4,3},{5,4},{6,5},{7,6},{0,7},{9,8},{10,9},{11,1... | collective-permute-start | bytes 1179656 | tf_op jit(solution)/shard_map/ppermute | solution.py:24
  107.1 16.5 %collective-permute-start.8 = (f32[3,128,1,256]{1,2,3,0:T(1,128)S(1)}, f32[3,128,1,256]{1,2,3,0:T(1,128)S(1)}, u32[]{:S(2)}, u32[]{:S(2)}) collective-permute-start(f32[3,128,1,256]{1,2,3,0:T(1,128)S(1)} %get-tuple-element.51), channel_id=1, source_target_pairs={{0,1},{1,2},{2,3},{3,4},{4,5},{5,6},{6,7},{7,0},{8,9},{9,10},{10,1... | collective-permute-start | bytes 1179656 | tf_op jit(solution)/shard_map/ppermute | solution.py:22
  107.2 18.7 %collective-permute-start.9 = (f32[3,128,1,256]{1,2,3,0:T(1,128)S(1)}, f32[3,128,1,256]{1,2,3,0:T(1,128)S(1)}, u32[]{:S(2)}, u32[]{:S(2)}) collective-permute-start(f32[3,128,1,256]{1,2,3,0:T(1,128)S(1)} %get-tuple-element.52), channel_id=1, source_target_pairs={{1,0},{2,1},{3,2},{4,3},{5,4},{6,5},{7,6},{0,7},{9,8},{10,9},{11,1... | collective-permute-start | bytes 1179656 | tf_op jit(solution)/shard_map/ppermute | solution.py:24
  129.7 15.8 %collective-permute-start.10 = (f32[3,128,1,256]{1,2,3,0:T(1,128)S(1)}, f32[3,128,1,256]{1,2,3,0:T(1,128)S(1)}, u32[]{:S(2)}, u32[]{:S(2)}) collective-permute-start(f32[3,128,1,256]{1,2,3,0:T(1,128)S(1)} %get-tuple-element.49), channel_id=1, source_target_pairs={{0,1},{1,2},{2,3},{3,4},{4,5},{5,6},{6,7},{7,0},{8,9},{9,10},{10,1... | collective-permute-start | bytes 1179656 | tf_op jit(solution)/shard_map/ppermute | solution.py:22
  130.0 20.2 %collective-permute-start.11 = (f32[3,128,1,256]{1,2,3,0:T(1,128)S(1)}, f32[3,128,1,256]{1,2,3,0:T(1,128)S(1)}, u32[]{:S(2)}, u32[]{:S(2)}) collective-permute-start(f32[3,128,1,256]{1,2,3,0:T(1,128)S(1)} %get-tuple-element.50), channel_id=1, source_target_pairs={{1,0},{2,1},{3,2},{4,3},{5,4},{6,5},{7,6},{0,7},{9,8},{10,9},{11,1... | collective-permute-start | bytes 1179656 | tf_op jit(solution)/shard_map/ppermute | solution.py:24
  157.3 17.2 %collective-permute-start.12 = (f32[3,128,1,256]{1,2,3,0:T(1,128)S(1)}, f32[3,128,1,256]{1,2,3,0:T(1,128)S(1)}, u32[]{:S(2)}, u32[]{:S(2)}) collective-permute-start(f32[3,128,1,256]{1,2,3,0:T(1,128)S(1)} %get-tuple-element.47), channel_id=1, source_target_pairs={{0,1},{1,2},{2,3},{3,4},{4,5},{5,6},{6,7},{7,0},{8,9},{9,10},{10,1... | collective-permute-start | bytes 1179656 | tf_op jit(solution)/shard_map/ppermute | solution.py:22
  157.3 19.8 %collective-permute-start.13 = (f32[3,128,1,256]{1,2,3,0:T(1,128)S(1)}, f32[3,128,1,256]{1,2,3,0:T(1,128)S(1)}, u32[]{:S(2)}, u32[]{:S(2)}) collective-permute-start(f32[3,128,1,256]{1,2,3,0:T(1,128)S(1)} %get-tuple-element.48), channel_id=1, source_target_pairs={{1,0},{2,1},{3,2},{4,3},{5,4},{6,5},{7,6},{0,7},{9,8},{10,9},{11,1... | collective-permute-start | bytes 1179656 | tf_op jit(solution)/shard_map/ppermute | solution.py:24
  181.0 16.5 %collective-permute-start.14 = (f32[3,128,1,256]{1,2,3,0:T(1,128)S(1)}, f32[3,128,1,256]{1,2,3,0:T(1,128)S(1)}, u32[]{:S(2)}, u32[]{:S(2)}) collective-permute-start(f32[3,128,1,256]{1,2,3,0:T(1,128)S(1)} %get-tuple-element.45), channel_id=1, source_target_pairs={{0,1},{1,2},{2,3},{3,4},{4,5},{5,6},{6,7},{7,0},{8,9},{9,10},{10,1... | collective-permute-start | bytes 1179656 | tf_op jit(solution)/shard_map/ppermute | solution.py:22
  181.1 20.5 %collective-permute-start.15 = (f32[3,128,1,256]{1,2,3,0:T(1,128)S(1)}, f32[3,128,1,256]{1,2,3,0:T(1,128)S(1)}, u32[]{:S(2)}, u32[]{:S(2)}) collective-permute-start(f32[3,128,1,256]{1,2,3,0:T(1,128)S(1)} %get-tuple-element.46), channel_id=1, source_target_pairs={{1,0},{2,1},{3,2},{4,3},{5,4},{6,5},{7,6},{0,7},{9,8},{10,9},{11,1... | collective-permute-start | bytes 1179656 | tf_op jit(solution)/shard_map/ppermute | solution.py:24
  209.8 40.7 %all-to-all-start = ((f32[3,128,8,256]{1,2,0,3:T(8,128)}), f32[3,128,8,256]{1,2,0,3:T(8,128)S(1)}, u32[]{:S(2)}, u32[]{:S(2)}) async-start(f32[3,128,8,256]{1,2,0,3:T(8,128)} %pad_maximum_fusion.27), calls=%async_computation | async-start | bytes 6291456 | tf_op jit(solution)/shard_map/all_to_all | solution.py:94
  262.8 11.8 %collective-permute-start.17 = (f32[1,1,2,512,128]{3,4,2,1,0:T(8,128)S(1)}, f32[1,1,2,512,128]{3,4,2,1,0:T(8,128)S(1)}, u32[]{:S(2)}, u32[]{:S(2)}) collective-permute-start(f32[1,1,2,512,128]{3,4,2,1,0:T(8,128)S(1)} %maximum_bitcast_fusion), channel_id=1, source_target_pairs={{8,0},{16,8},{24,16},{0,24},{9,1},{17,9},{25,17},{1,25},{10,2},{18... | collective-permute-start | bytes 1572872 | tf_op jit(solution)/shard_map/ppermute | solution.py:24
  262.9 13.9 %collective-permute-start.16 = (f32[1,1,2,512,128]{3,4,2,1,0:T(8,128)S(1)}, f32[1,1,2,512,128]{3,4,2,1,0:T(8,128)S(1)}, u32[]{:S(2)}, u32[]{:S(2)}) collective-permute-start(f32[1,1,2,512,128]{3,4,2,1,0:T(8,128)S(1)} %maximum_bitcast_fusion), channel_id=1, source_target_pairs={{0,8},{8,16},{16,24},{24,0},{1,9},{9,17},{17,25},{25,1},{2,10},{10... | collective-permute-start | bytes 1572872 | tf_op jit(solution)/shard_map/ppermute | solution.py:22
  278.2 70.2 %collective-permute-start.19 = (f32[1,3,2,512,128]{3,4,2,1,0:T(8,128)}, f32[1,3,2,512,128]{3,4,2,1,0:T(8,128)}, u32[]{:S(2)}, u32[]{:S(2)}) collective-permute-start(f32[1,3,2,512,128]{3,4,2,1,0:T(8,128)} %pad_maximum_fusion.28), channel_id=1, source_target_pairs={{1,0},{2,1},{3,2},{4,3},{5,4},{6,5},{7,6},{0,7},{9,8},{10,9},{11,1... | collective-permute-start | bytes 4718600 | tf_op jit(solution)/shard_map/ppermute | solution.py:24
  279.6 68.8 %collective-permute-start.18 = (f32[1,3,2,512,128]{3,4,2,1,0:T(8,128)}, f32[1,3,2,512,128]{3,4,2,1,0:T(8,128)}, u32[]{:S(2)}, u32[]{:S(2)}) collective-permute-start(f32[1,3,2,512,128]{3,4,2,1,0:T(8,128)} %pad_maximum_fusion.28), channel_id=1, source_target_pairs={{0,1},{1,2},{2,3},{3,4},{4,5},{5,6},{6,7},{7,0},{8,9},{9,10},{10,1... | collective-permute-start | bytes 4718600 | tf_op jit(solution)/shard_map/ppermute | solution.py:22
  282.5 65.9 %copy-start.12 = (f32[1,1,2,512,128]{3,4,2,1,0:T(8,128)S(1)}, f32[1,1,2,512,128]{3,4,2,1,0:T(8,128)}, u32[]{:S(2)}) copy-start(f32[1,1,2,512,128]{3,4,2,1,0:T(8,128)} %copy-done.11) | copy-start | bytes 1572868
  282.5 65.9 %copy-start.14 = (f32[1,1,2,512,128]{3,4,2,1,0:T(8,128)S(1)}, f32[1,1,2,512,128]{3,4,2,1,0:T(8,128)}, u32[]{:S(2)}) copy-start(f32[1,1,2,512,128]{3,4,2,1,0:T(8,128)} %copy-done.13) | copy-start | bytes 1572868
  (17 other events, 201.9 us)
where the time goes:
time: 619 us; the launch traced here: 611 us
  waiting for transfers between devices  232 us (37%)
  other arithmetic  173 us (28%)
  local copies, waits for them, and re-layouts  82.7 us (13%)
  starting transfers between devices  46.8 us (8%)
  blocking collectives  40.7 us (7%)
  matrix products  31.9 us (5%)
    ppermute x10, waiting for transfers between devices, extended(): lax.ppermute(head, axis, [((i + 1) % count, i) for i in range(count)])  102 us
    ppermute x10, waiting for transfers between devices, extended(): lax.ppermute(tail, axis, [(i, (i + 1) % count) for i in range(count)])  96.8 us
    another operation x15, other arithmetic, analyse_tile(): factor = jnp.linalg.cholesky(gram)  79.6 us
    all_to_all x1, blocking collectives, local(): lax.all_to_all(updated, 'members', split_axis=1, concat_axis=3, tiled=True)  40.7 us
    another operation x3, other arithmetic, analyse_tile(): reduced = jax.scipy.linalg.cho_solve((factor, True), spread_all)  40.5 us
    ppermute x10, starting transfers between devices, extended(): lax.ppermute(head, axis, [((i + 1) % count, i) for i in range(count)])  38 us
    all_to_all x1, waiting for transfers between devices, local(): lax.all_to_all(state, 'members', split_axis=3, concat_axis=1, tiled=True)  33.3 us
    another operation x15, other arithmetic, local(): state = jnp.stack([eta_new, east, north])  18.8 us
  transfers between devices with their start and end apart: 21, of which 20 were waited for; matrix products, arithmetic and copies ran while one was open for 1% of the time, Pallas kernels for 0%

commit v1 on v0

--- a/solution.py
+++ b/solution.py
@@ -10,6 +10,15 @@
 depth = 1.0
 coriolis = 0.25
 viscosity = 0.5
+
+
+def _track_boxes(inner_x):
+    block_now = lax.axis_size("members")
+    k_now = jnp.split(inner_x, block_now, axis=3)
+    met_up = jnp.stack(k_now, axis=0)
+    low = lax.all_to_all(met_up, axis_name="members", split_axis=0, concat_axis=0)
+    block_next = jnp.concatenate(low, axis=1)
+    return block_next
 
 
 def extended(cells, sides, width):
@@ -91,7 +100,7 @@
         east, north = momentum_update(padded[0], padded[1], padded[2])
         state = jnp.stack([eta_new, east, north])
     width = TILE_W
-    tiles = lax.all_to_all(state, "members", split_axis=3, concat_axis=1, tiled=True)
+    tiles = _track_boxes(state)
     count = tiles.shape[1]
     rows_here = tiles.shape[2]
     tile = tiles.reshape(3, count, rows_here * width)

time: 619 us -> 620 us (level)
  other arithmetic: 173 us -> 163 us
  local copies, waits for them, and re-layouts: 82.7 us -> 90.5 us
    another operation x12 -> x15, local copies, waits for them, and re-layouts: 10.6 us -> 22.7 us
    concatenate x10 -> x9, other arithmetic: 15 us -> 6.61 us  [extended(): jnp.concatenate([lax.ppermute(tail, axis, [(i, (i + 1) % count) for i in...]
    slice x30, local copies, waits for them, and re-layouts: 4.53 us -> 10.9 us  [centred_x(): return 0.5 * (jnp.roll(field, -1, axis=2) - jnp.roll(field, 1, axis=2))]
    unnamed x43 -> x41, local copies, waits for them, and re-layouts: 18.1 us -> 16.2 us
    another operation x15 -> x16, other arithmetic: 18.8 us -> 18.9 us  [local(): state = jnp.stack([eta_new, east, north])]
where the time goes in v1:
time: 620 us; the launch traced here: 611 us
  waiting for transfers between devices  235 us (38%)
  other arithmetic  163 us (26%)
  local copies, waits for them, and re-layouts  90.5 us (15%)
  starting transfers between devices  46.5 us (8%)
  blocking collectives  40.8 us (7%)
  matrix products  31.7 us (5%)
    ppermute x10, waiting for transfers between devices, extended(): lax.ppermute(head, axis, [((i + 1) % count, i) for i in range(count)])  105 us
    ppermute x10, waiting for transfers between devices, extended(): lax.ppermute(tail, axis, [(i, (i + 1) % count) for i in range(count)])  96.7 us
    another operation x15, other arithmetic, analyse_tile(): factor = jnp.linalg.cholesky(gram)  79.6 us
    all_to_all x1, blocking collectives, local(): lax.all_to_all(updated, 'members', split_axis=1, concat_axis=3, tiled=True)  40.8 us
    another operation x3, other arithmetic, analyse_tile(): reduced = jax.scipy.linalg.cho_solve((factor, True), spread_all)  40.4 us
    ppermute x10, starting transfers between devices, extended(): lax.ppermute(head, axis, [((i + 1) % count, i) for i in range(count)])  35.9 us
    all_to_all x1, waiting for transfers between devices, _track_boxes(): lax.all_to_all(met_up, axis_name='members', split_axis=0, concat_axis=0)  33.3 us
    another operation x16, other arithmetic, local(): state = jnp.stack([eta_new, east, north])  18.9 us
  transfers between devices with their start and end apart: 21, of which 20 were waited for; matrix products, arithmetic and copies ran while one was open for 1% of the time, Pallas kernels for 0%

profile of v1, /device:TPU:0, one launch (start us, length us, event | category | flops | bytes accessed | tf_op | source)
XLA Modules:
  0.0 611.2 jit_solution(14675533651286494859)
XLA Ops:
  10.3 13.0 %collective-permute-done = f32[3,128,1,256]{3,1,2,0:T(8,128)S(1)} collective-permute-done((f32[3,128,1,256]{3,1,2,0:T(8,128)S(1)}, f32[3,128,1,256]{3,1,2,0:T(8,128)S(1)}, u32[]{:S(2)}, u32[]{:S(2)}) %collective-permute-start) | collective-permute-done | bytes 393248 | tf_op jit(solution)/shard_map/ppermute | solution.py:31
  32.2 12.4 %collective-permute-done.2 = f32[3,128,1,256]{3,1,2,0:T(8,128)S(1)} collective-permute-done((f32[3,128,1,256]{3,1,2,0:T(8,128)S(1)}, f32[3,128,1,256]{3,1,2,0:T(8,128)S(1)}, u32[]{:S(2)}, u32[]{:S(2)}) %collective-permute-start.2) | collective-permute-done | bytes 393248 | tf_op jit(solution)/shard_map/ppermute | solution.py:31
  59.4 11.7 %collective-permute-done.4 = f32[3,128,1,256]{3,1,2,0:T(8,128)S(1)} collective-permute-done((f32[3,128,1,256]{3,1,2,0:T(8,128)S(1)}, f32[3,128,1,256]{3,1,2,0:T(8,128)S(1)}, u32[]{:S(2)}, u32[]{:S(2)}) %collective-permute-start.4) | collective-permute-done | bytes 393248 | tf_op jit(solution)/shard_map/ppermute | solution.py:31
  82.4 11.5 %collective-permute-done.6 = f32[3,128,1,256]{3,1,2,0:T(8,128)S(1)} collective-permute-done((f32[3,128,1,256]{3,1,2,0:T(8,128)S(1)}, f32[3,128,1,256]{3,1,2,0:T(8,128)S(1)}, u32[]{:S(2)}, u32[]{:S(2)}) %collective-permute-start.6) | collective-permute-done | bytes 393248 | tf_op jit(solution)/shard_map/ppermute | solution.py:31
  109.8 11.8 %collective-permute-done.8 = f32[3,128,1,256]{3,1,2,0:T(8,128)S(1)} collective-permute-done((f32[3,128,1,256]{3,1,2,0:T(8,128)S(1)}, f32[3,128,1,256]{3,1,2,0:T(8,128)S(1)}, u32[]{:S(2)}, u32[]{:S(2)}) %collective-permute-start.8) | collective-permute-done | bytes 393248 | tf_op jit(solution)/shard_map/ppermute | solution.py:31
  131.2 11.0 %collective-permute-done.10 = f32[3,128,1,256]{3,1,2,0:T(8,128)S(1)} collective-permute-done((f32[3,128,1,256]{3,1,2,0:T(8,128)S(1)}, f32[3,128,1,256]{3,1,2,0:T(8,128)S(1)}, u32[]{:S(2)}, u32[]{:S(2)}) %collective-permute-start.10) | collective-permute-done | bytes 393248 | tf_op jit(solution)/shard_map/ppermute | solution.py:31
  157.3 10.5 %collective-permute-done.12 = f32[3,128,1,256]{3,1,2,0:T(8,128)S(1)} collective-permute-done((f32[3,128,1,256]{3,1,2,0:T(8,128)S(1)}, f32[3,128,1,256]{3,1,2,0:T(8,128)S(1)}, u32[]{:S(2)}, u32[]{:S(2)}) %collective-permute-start.12) | collective-permute-done | bytes 393248 | tf_op jit(solution)/shard_map/ppermute | solution.py:31
  179.9 12.5 %collective-permute-done.14 = f32[3,128,1,256]{3,1,2,0:T(8,128)S(1)} collective-permute-done((f32[3,128,1,256]{3,1,2,0:T(8,128)S(1)}, f32[3,128,1,256]{3,1,2,0:T(8,128)S(1)}, u32[]{:S(2)}, u32[]{:S(2)}) %collective-permute-start.14) | collective-permute-done | bytes 393248 | tf_op jit(solution)/shard_map/ppermute | solution.py:31
  220.0 33.3 %all-to-all-done = f32[4,3,128,8,64]{2,4,3,1,0:T(8,128)S(1)} async-done(((f32[4,3,128,8,64]{2,4,3,1,0:T(8,128)}), f32[4,3,128,8,64]{2,4,3,1,0:T(8,128)S(1)}, u32[]{:S(2)}, u32[]{:S(2)}) %all-to-all-start) | async-done | bytes 3145760 | tf_op jit(solution)/shard_map/all_to_all | solution.py:19
  266.7 11.2 %collective-permute-done.17 = f32[1,1,2,512,128]{3,4,2,1,0:T(8,128)S(1)} collective-permute-done((f32[1,1,2,512,128]{3,4,2,1,0:T(8,128)S(1)}, f32[1,1,2,512,128]{3,4,2,1,0:T(8,128)S(1)}, u32[]{:S(2)}, u32[]{:S(2)}) %collective-permute-start.17) | collective-permute-done | bytes 524320 | tf_op jit(solution)/shard_map/ppermute | solution.py:33
  284.0 67.8 %collective-permute-done.19 = f32[1,3,2,512,128]{3,4,2,1,0:T(8,128)} collective-permute-done((f32[1,3,2,512,128]{3,4,2,1,0:T(8,128)}, f32[1,3,2,512,128]{3,4,2,1,0:T(8,128)}, u32[]{:S(2)}, u32[]{:S(2)}) %collective-permute-start.19) | collective-permute-done | bytes 1572896 | tf_op jit(solution)/shard_map/ppermute | solution.py:33
  369.9 11.7 %cholesky.104 = f32[128,128]{1,0:T(8,128)S(1)} custom-call(f32[128,128]{1,0:T(8,128)S(1)} %cholesky.266), custom_call_target="Cholesky" | custom-call | tf_op jit(solution)/shard_map/jit(cholesky)/cholesky | solution.py:88
  382.3 10.0 %custom-call.34 = f32[1,128,128]{1,2,0:T(8,128)S(1)} custom-call(f32[1,128,128]{2,1,0:T(8,128)S(1)} %get-tuple-element.144), custom_call_target="InvertDiagBlocksLowerTriangular" | custom-call | tf_op jit(solution)/shard_map/jit(cholesky)/cholesky | solution.py:88
  396.3 11.7 %cholesky.217 = f32[128,128]{1,0:T(8,128)S(1)} custom-call(f32[128,128]{1,0:T(8,128)S(1)} %cholesky.270), custom_call_target="Cholesky" | custom-call | tf_op jit(solution)/shard_map/jit(cholesky)/cholesky | solution.py:88
  408.8 9.8 %custom-call.35 = f32[1,128,128]{1,2,0:T(8,128)S(1)} custom-call(f32[1,128,128]{2,1,0:T(8,128)S(1)} %get-tuple-element.141), custom_call_target="InvertDiagBlocksLowerTriangular" | custom-call | tf_op jit(solution)/shard_map/jit(cholesky)/cholesky | solution.py:88
  419.3 11.7 %cholesky.238 = f32[128,128]{1,0:T(8,128)S(1)} custom-call(f32[128,128]{1,0:T(8,128)S(1)} %cholesky.275), custom_call_target="Cholesky" | custom-call | tf_op jit(solution)/shard_map/jit(cholesky)/cholesky | solution.py:88
  431.6 10.2 %custom-call.36 = f32[1,128,128]{1,2,0:T(8,128)S(1)} custom-call(f32[1,128,128]{2,1,0:T(8,128)S(1)} %get-tuple-element.138), custom_call_target="InvertDiagBlocksLowerTriangular" | custom-call | tf_op jit(solution)/shard_map/jit(cholesky)/cholesky | solution.py:88
  442.4 11.7 %cholesky.255 = f32[128,128]{1,0:T(8,128)S(1)} custom-call(f32[128,128]{1,0:T(8,128)S(1)} %convolution_subtract_fusion.8), custom_call_target="Cholesky" | custom-call | tf_op jit(solution)/shard_map/jit(cholesky)/cholesky | solution.py:88
  457.4 10.4 %while.1 = (s32[]{:T(128)}, f32[512,512]{1,0:T(8,128)S(1)}, s32[4,2]{0,1:T(2,128)S(1)}, f32[4,128,128]{2,1,0:T(8,128)}, s32[]{:T(128)}) while((s32[]{:T(128)}, f32[512,512]{1,0:T(8,128)S(1)}, s32[4,2]{0,1:T(2,128)S(1)}, f32[4,128,128]{2,1,0:T(8,128)}, s32[]{:T(128)}) %tuple.93), condition=%wide.while_cond, body=%wide.while_body.sunk | while | flops 2 | bytes 132205 | solution.py:89
  467.9 40.3 %custom-call.37 = f32[4,128,128]{1,2,0:T(8,128)S(1)} custom-call(f32[4,128,128]{2,1,0:T(8,128)} %get-tuple-element.12), custom_call_target="InvertDiagBlocksLowerTriangular" | custom-call | tf_op jit(solution)/shard_map/jit(_cho_solve)/triangular_solve | solution.py:89
  533.4 7.0 %reshape.131 = f32[4,1,196608]{2,1,0:T(1,128)} reshape(f32[512,3,8,64]{3,2,1,0:T(8,128)} %bitcast.227) | data formatting | bytes 6291456
  540.4 40.8 %all_to_all.23 = f32[4,1,196608]{2,1,0:T(1,128)S(1)} all-to-all(f32[4,1,196608]{2,1,0:T(1,128)} %reshape.131), channel_id=1, replica_groups=mesh['members'=4,'space'=8] {'members'}, dimensions={0} | all-to-all | bytes 6291456 | tf_op jit(solution)/shard_map/all_to_all | solution.py:125
  581.8 10.6 %reduce.25 = f32[4,196608]{1,0:T(4,128)} reduce(f32[4,1,196608]{2,1,0:T(1,128)S(1)} %all_to_all.23, f32[]{:T(128)} %broadcast.379), dimensions={1}, to_apply=%all_to_all.17.reduce_sub_computation | reduce | bytes 6291460 | tf_op jit(solution)/shard_map/all_to_all | solution.py:125
  592.5 7.4 %reshape.132 = f32[512,3,8,64]{3,2,1,0:T(8,128)} reshape(f32[4,196608]{1,0:T(4,128)} %reduce.25) | data formatting | bytes 6291456
  (233 shorter events, 217.3 us)
Async XLA Ops:
  0.0 216.5 %copy-start = (f32[512,1,1,128]{3,2,1,0:T(1,128)S(1)}, f32[512,1,1,128]{3,2,1,0:T(1,128)}, u32[]{:S(2)}) copy-start(f32[512,1,1,128]{3,2,1,0:T(1,128)} %param.10) | copy-start | bytes 786436
  3.5 19.8 %collective-permute-start = (f32[3,128,1,256]{3,1,2,0:T(8,128)S(1)}, f32[3,128,1,256]{3,1,2,0:T(8,128)S(1)}, u32[]{:S(2)}, u32[]{:S(2)}) collective-permute-start(f32[3,128,1,256]{3,1,2,0:T(8,128)S(1)} %copy.77), channel_id=1, source_target_pairs={{0,1},{1,2},{2,3},{3,4},{4,5},{5,6},{6,7},{7,0},{8,9},{9,10},{10,1... | collective-permute-start | bytes 1179656 | tf_op jit(solution)/shard_map/ppermute | solution.py:31
  6.6 19.1 %collective-permute-start.1 = (f32[3,128,1,256]{3,1,2,0:T(8,128)S(1)}, f32[3,128,1,256]{3,1,2,0:T(8,128)S(1)}, u32[]{:S(2)}, u32[]{:S(2)}) collective-permute-start(f32[3,128,1,256]{3,1,2,0:T(8,128)S(1)} %copy.78), channel_id=1, source_target_pairs={{1,0},{2,1},{3,2},{4,3},{5,4},{6,5},{7,6},{0,7},{9,8},{10,9},{11,1... | collective-permute-start | bytes 1179656 | tf_op jit(solution)/shard_map/ppermute | solution.py:33
  27.4 17.2 %collective-permute-start.2 = (f32[3,128,1,256]{3,1,2,0:T(8,128)S(1)}, f32[3,128,1,256]{3,1,2,0:T(8,128)S(1)}, u32[]{:S(2)}, u32[]{:S(2)}) collective-permute-start(f32[3,128,1,256]{3,1,2,0:T(8,128)S(1)} %get-tuple-element.61), channel_id=1, source_target_pairs={{0,1},{1,2},{2,3},{3,4},{4,5},{5,6},{6,7},{7,0},{8,9},{9,10},{10,1... | collective-permute-start | bytes 1179656 | tf_op jit(solution)/shard_map/ppermute | solution.py:31
  28.6 18.9 %collective-permute-start.3 = (f32[3,128,1,256]{3,1,2,0:T(8,128)S(1)}, f32[3,128,1,256]{3,1,2,0:T(8,128)S(1)}, u32[]{:S(2)}, u32[]{:S(2)}) collective-permute-start(f32[3,128,1,256]{3,1,2,0:T(8,128)S(1)} %get-tuple-element.62), channel_id=1, source_target_pairs={{1,0},{2,1},{3,2},{4,3},{5,4},{6,5},{7,6},{0,7},{9,8},{10,9},{11,1... | collective-permute-start | bytes 1179656 | tf_op jit(solution)/shard_map/ppermute | solution.py:33
  54.6 16.5 %collective-permute-start.4 = (f32[3,128,1,256]{3,1,2,0:T(8,128)S(1)}, f32[3,128,1,256]{3,1,2,0:T(8,128)S(1)}, u32[]{:S(2)}, u32[]{:S(2)}) collective-permute-start(f32[3,128,1,256]{3,1,2,0:T(8,128)S(1)} %get-tuple-element.59), channel_id=1, source_target_pairs={{0,1},{1,2},{2,3},{3,4},{4,5},{5,6},{6,7},{7,0},{8,9},{9,10},{10,1... | collective-permute-start | bytes 1179656 | tf_op jit(solution)/shard_map/ppermute | solution.py:31
  54.7 20.3 %collective-permute-start.5 = (f32[3,128,1,256]{3,1,2,0:T(8,128)S(1)}, f32[3,128,1,256]{3,1,2,0:T(8,128)S(1)}, u32[]{:S(2)}, u32[]{:S(2)}) collective-permute-start(f32[3,128,1,256]{3,1,2,0:T(8,128)S(1)} %get-tuple-element.60), channel_id=1, source_target_pairs={{1,0},{2,1},{3,2},{4,3},{5,4},{6,5},{7,6},{0,7},{9,8},{10,9},{11,1... | collective-permute-start | bytes 1179656 | tf_op jit(solution)/shard_map/ppermute | solution.py:33
  77.5 16.5 %collective-permute-start.6 = (f32[3,128,1,256]{3,1,2,0:T(8,128)S(1)}, f32[3,128,1,256]{3,1,2,0:T(8,128)S(1)}, u32[]{:S(2)}, u32[]{:S(2)}) collective-permute-start(f32[3,128,1,256]{3,1,2,0:T(8,128)S(1)} %get-tuple-element.57), channel_id=1, source_target_pairs={{0,1},{1,2},{2,3},{3,4},{4,5},{5,6},{6,7},{7,0},{8,9},{9,10},{10,1... | collective-permute-start | bytes 1179656 | tf_op jit(solution)/shard_map/ppermute | solution.py:31
  77.5 20.5 %collective-permute-start.7 = (f32[3,128,1,256]{3,1,2,0:T(8,128)S(1)}, f32[3,128,1,256]{3,1,2,0:T(8,128)S(1)}, u32[]{:S(2)}, u32[]{:S(2)}) collective-permute-start(f32[3,128,1,256]{3,1,2,0:T(8,128)S(1)} %get-tuple-element.58), channel_id=1, source_target_pairs={{1,0},{2,1},{3,2},{4,3},{5,4},{6,5},{7,6},{0,7},{9,8},{10,9},{11,1... | collective-permute-start | bytes 1179656 | tf_op jit(solution)/shard_map/ppermute | solution.py:33
  105.1 16.5 %collective-permute-start.8 = (f32[3,128,1,256]{3,1,2,0:T(8,128)S(1)}, f32[3,128,1,256]{3,1,2,0:T(8,128)S(1)}, u32[]{:S(2)}, u32[]{:S(2)}) collective-permute-start(f32[3,128,1,256]{3,1,2,0:T(8,128)S(1)} %get-tuple-element.55), channel_id=1, source_target_pairs={{0,1},{1,2},{2,3},{3,4},{4,5},{5,6},{6,7},{7,0},{8,9},{9,10},{10,1... | collective-permute-start | bytes 1179656 | tf_op jit(solution)/shard_map/ppermute | solution.py:31
  105.1 18.9 %collective-permute-start.9 = (f32[3,128,1,256]{3,1,2,0:T(8,128)S(1)}, f32[3,128,1,256]{3,1,2,0:T(8,128)S(1)}, u32[]{:S(2)}, u32[]{:S(2)}) collective-permute-start(f32[3,128,1,256]{3,1,2,0:T(8,128)S(1)} %get-tuple-element.56), channel_id=1, source_target_pairs={{1,0},{2,1},{3,2},{4,3},{5,4},{6,5},{7,6},{0,7},{9,8},{10,9},{11,1... | collective-permute-start | bytes 1179656 | tf_op jit(solution)/shard_map/ppermute | solution.py:33
  126.4 15.8 %collective-permute-start.10 = (f32[3,128,1,256]{3,1,2,0:T(8,128)S(1)}, f32[3,128,1,256]{3,1,2,0:T(8,128)S(1)}, u32[]{:S(2)}, u32[]{:S(2)}) collective-permute-start(f32[3,128,1,256]{3,1,2,0:T(8,128)S(1)} %get-tuple-element.53), channel_id=1, source_target_pairs={{0,1},{1,2},{2,3},{3,4},{4,5},{5,6},{6,7},{7,0},{8,9},{9,10},{10,1... | collective-permute-start | bytes 1179656 | tf_op jit(solution)/shard_map/ppermute | solution.py:31
  126.5 18.6 %collective-permute-start.11 = (f32[3,128,1,256]{3,1,2,0:T(8,128)S(1)}, f32[3,128,1,256]{3,1,2,0:T(8,128)S(1)}, u32[]{:S(2)}, u32[]{:S(2)}) collective-permute-start(f32[3,128,1,256]{3,1,2,0:T(8,128)S(1)} %get-tuple-element.54), channel_id=1, source_target_pairs={{1,0},{2,1},{3,2},{4,3},{5,4},{6,5},{7,6},{0,7},{9,8},{10,9},{11,1... | collective-permute-start | bytes 1179656 | tf_op jit(solution)/shard_map/ppermute | solution.py:33
  152.2 15.6 %collective-permute-start.12 = (f32[3,128,1,256]{3,1,2,0:T(8,128)S(1)}, f32[3,128,1,256]{3,1,2,0:T(8,128)S(1)}, u32[]{:S(2)}, u32[]{:S(2)}) collective-permute-start(f32[3,128,1,256]{3,1,2,0:T(8,128)S(1)} %get-tuple-element.51), channel_id=1, source_target_pairs={{0,1},{1,2},{2,3},{3,4},{4,5},{5,6},{6,7},{7,0},{8,9},{9,10},{10,1... | collective-permute-start | bytes 1179656 | tf_op jit(solution)/shard_map/ppermute | solution.py:31
  152.2 20.4 %collective-permute-start.13 = (f32[3,128,1,256]{3,1,2,0:T(8,128)S(1)}, f32[3,128,1,256]{3,1,2,0:T(8,128)S(1)}, u32[]{:S(2)}, u32[]{:S(2)}) collective-permute-start(f32[3,128,1,256]{3,1,2,0:T(8,128)S(1)} %get-tuple-element.52), channel_id=1, source_target_pairs={{1,0},{2,1},{3,2},{4,3},{5,4},{6,5},{7,6},{0,7},{9,8},{10,9},{11,1... | collective-permute-start | bytes 1179656 | tf_op jit(solution)/shard_map/ppermute | solution.py:33
  175.1 17.3 %collective-permute-start.14 = (f32[3,128,1,256]{3,1,2,0:T(8,128)S(1)}, f32[3,128,1,256]{3,1,2,0:T(8,128)S(1)}, u32[]{:S(2)}, u32[]{:S(2)}) collective-permute-start(f32[3,128,1,256]{3,1,2,0:T(8,128)S(1)} %get-tuple-element.49), channel_id=1, source_target_pairs={{0,1},{1,2},{2,3},{3,4},{4,5},{5,6},{6,7},{7,0},{8,9},{9,10},{10,1... | collective-permute-start | bytes 1179656 | tf_op jit(solution)/shard_map/ppermute | solution.py:31
  175.2 20.3 %collective-permute-start.15 = (f32[3,128,1,256]{3,1,2,0:T(8,128)S(1)}, f32[3,128,1,256]{3,1,2,0:T(8,128)S(1)}, u32[]{:S(2)}, u32[]{:S(2)}) collective-permute-start(f32[3,128,1,256]{3,1,2,0:T(8,128)S(1)} %get-tuple-element.50), channel_id=1, source_target_pairs={{1,0},{2,1},{3,2},{4,3},{5,4},{6,5},{7,6},{0,7},{9,8},{10,9},{11,1... | collective-permute-start | bytes 1179656 | tf_op jit(solution)/shard_map/ppermute | solution.py:33
  212.7 40.7 %all-to-all-start = ((f32[4,3,128,8,64]{2,4,3,1,0:T(8,128)}), f32[4,3,128,8,64]{2,4,3,1,0:T(8,128)S(1)}, u32[]{:S(2)}, u32[]{:S(2)}) async-start(f32[4,3,128,8,64]{2,4,3,1,0:T(8,128)} %copy.50), calls=%async_computation | async-start | bytes 6291456 | tf_op jit(solution)/shard_map/all_to_all | solution.py:19
  266.2 11.8 %collective-permute-start.17 = (f32[1,1,2,512,128]{3,4,2,1,0:T(8,128)S(1)}, f32[1,1,2,512,128]{3,4,2,1,0:T(8,128)S(1)}, u32[]{:S(2)}, u32[]{:S(2)}) collective-permute-start(f32[1,1,2,512,128]{3,4,2,1,0:T(8,128)S(1)} %maximum_bitcast_fusion), channel_id=1, source_target_pairs={{8,0},{16,8},{24,16},{0,24},{9,1},{17,9},{25,17},{1,25},{10,2},{18... | collective-permute-start | bytes 1572872 | tf_op jit(solution)/shard_map/ppermute | solution.py:33
  266.3 13.9 %collective-permute-start.16 = (f32[1,1,2,512,128]{3,4,2,1,0:T(8,128)S(1)}, f32[1,1,2,512,128]{3,4,2,1,0:T(8,128)S(1)}, u32[]{:S(2)}, u32[]{:S(2)}) collective-permute-start(f32[1,1,2,512,128]{3,4,2,1,0:T(8,128)S(1)} %maximum_bitcast_fusion), channel_id=1, source_target_pairs={{0,8},{8,16},{16,24},{24,0},{1,9},{9,17},{17,25},{25,1},{2,10},{10... | collective-permute-start | bytes 1572872 | tf_op jit(solution)/shard_map/ppermute | solution.py:31
  281.5 70.2 %collective-permute-start.19 = (f32[1,3,2,512,128]{3,4,2,1,0:T(8,128)}, f32[1,3,2,512,128]{3,4,2,1,0:T(8,128)}, u32[]{:S(2)}, u32[]{:S(2)}) collective-permute-start(f32[1,3,2,512,128]{3,4,2,1,0:T(8,128)} %pad_maximum_fusion.28), channel_id=1, source_target_pairs={{1,0},{2,1},{3,2},{4,3},{5,4},{6,5},{7,6},{0,7},{9,8},{10,9},{11,1... | collective-permute-start | bytes 4718600 | tf_op jit(solution)/shard_map/ppermute | solution.py:33
  282.0 69.8 %collective-permute-start.18 = (f32[1,3,2,512,128]{3,4,2,1,0:T(8,128)}, f32[1,3,2,512,128]{3,4,2,1,0:T(8,128)}, u32[]{:S(2)}, u32[]{:S(2)}) collective-permute-start(f32[1,3,2,512,128]{3,4,2,1,0:T(8,128)} %pad_maximum_fusion.28), channel_id=1, source_target_pairs={{0,1},{1,2},{2,3},{3,4},{4,5},{5,6},{6,7},{7,0},{8,9},{9,10},{10,1... | collective-permute-start | bytes 4718600 | tf_op jit(solution)/shard_map/ppermute | solution.py:31
  369.9 24.6 %copy-start.5 = (f32[128,3,3,128]{0,3,2,1:T(8,128)S(1)}, f32[128,3,3,128]{0,3,2,1:T(8,128)}, u32[]{:S(2)}) copy-start(f32[128,3,3,128]{0,3,2,1:T(8,128)} %get-tuple-element.68) | copy-start | bytes 1769476
  457.4 51.5 %copy-start.7 = (f32[128,1152]{1,0:T(8,128)S(1)}, f32[128,1152]{1,0:T(8,128)}, u32[]{:S(2)}) copy-start(f32[128,1152]{1,0:T(8,128)} %copy.58) | copy-start | bytes 1769476
  (15 other events, 66.2 us)
